TPU v7x, 32 devices: a whole 2x2x4 slice. The times are simulated.
32 devices in a mesh: level: 4 (over x, core), gx: 2 (over y), gy: 4 (over z).
Axes of the slice: x: 2, y: 2, z: 4, core: 2. Of those that a mesh axis runs over, the one named last changes fastest.
Arguments:
- initial: float32 [8, 128, 512], P('gx', 'gy'), may hold values from -1 to 1
- mobility: float32 [8, 128, 512], P('gx', 'gy'), may hold values from 0.5 to 1.5
Outputs:
- finals: float32 [4, 8, 128, 512], P('level', 'gx', 'gy')
All inputs are finite; a program needn't handle non-finite values.
Results may differ from a plain program's by a relative error of at most 0.00002.
Values sent between devices are 32-bit elements; how exact they have to be, the bound alone decides.
A program may use at most 64 MiB of HBM per device.

v0:
```python
import jax
import jax.numpy as jnp
from jax import lax
from jax.sharding import PartitionSpec as P

STEPS = 5


time_step = 0.004
gradient_energy = 1.0


def padded_2(cells, sides, width):
    for axis, dim in sides:
        count = lax.axis_size(axis)
        head = lax.slice_in_dim(cells, 0, width, axis=dim)
        tail = lax.slice_in_dim(cells, cells.shape[dim] - width, cells.shape[dim], axis=dim)
        cells = jnp.concatenate(
            [
                lax.ppermute(tail, axis, [(i, (i + 1) % count) for i in range(count)]),
                cells,
                lax.ppermute(head, axis, [((i + 1) % count, i) for i in range(count)]),
            ],
            axis=dim,
        )
    return cells


def passed_along(shard, axis, by):
    count = lax.axis_size(axis)
    pairs = [(i, i + by) for i in range(count) if 0 <= i + by < count]
    return lax.ppermute(shard, axis, pairs)


def basis_integral(member, count_points, start_point, end_point):
    poly_terms = [1.0]
    denominator = 1.0
    for partner in range(count_points):
        if partner != member:
            widened = [0.0] * (len(poly_terms) + 1)
            for degree in range(len(poly_terms)):
                widened[degree + 1] += poly_terms[degree]
                widened[degree] -= partner * poly_terms[degree]
            poly_terms = widened
            denominator = denominator * (member - partner)
    integral = 0.0
    for degree in range(len(poly_terms)):
        integral += (
            poly_terms[degree]
            * (end_point ** (degree + 1) - start_point ** (degree + 1))
            / (degree + 1)
        )
    return integral / denominator


def quadrature_rows(count_steps):
    weights = [[0.0] * (count_steps + 1) for interval in range(count_steps)]
    for interval in range(count_steps):
        for member in range(interval + 2):
            weights[interval][member] = basis_integral(
                member, interval + 2, 1.0 * interval, 1.0 * interval + 1.0
            )
        weights[interval][interval] -= 1.0
    return weights


def extend(concentration):
    return padded_2(concentration, (("gx", 0), ("gy", 1)), 2)


def face_table(mobility):
    padded = padded_2(mobility, (("gx", 0), ("gy", 1)), 1)
    centre = padded[1:-1, 1:-1]
    x_plus = 0.5 * (centre + padded[2:, 1:-1])
    x_minus = 0.5 * (centre + padded[:-2, 1:-1])
    y_plus = 0.5 * (centre + padded[1:-1, 2:])
    y_minus = 0.5 * (centre + padded[1:-1, :-2])
    z_plus = 0.5 * (centre + jnp.roll(centre, -1, 2))
    z_minus = 0.5 * (centre + jnp.roll(centre, 1, 2))
    return (x_plus, x_minus, y_plus, y_minus, z_plus, z_minus)


def tendency_local(padded, faces):
    centre = padded[1:-1, 1:-1]
    laplace = -6.0 * centre
    laplace = laplace + padded[2:, 1:-1] + padded[:-2, 1:-1]
    laplace = laplace + padded[1:-1, 2:] + padded[1:-1, :-2]
    laplace = laplace + jnp.roll(centre, 1, 2) + jnp.roll(centre, -1, 2)
    potential = centre * centre * centre - centre - gradient_energy * laplace
    inner = potential[1:-1, 1:-1]
    result = faces[0] * (potential[2:, 1:-1] - inner) - faces[1] * (inner - potential[:-2, 1:-1])
    result = (
        result
        + faces[2] * (potential[1:-1, 2:] - inner)
        - faces[3] * (inner - potential[1:-1, :-2])
    )
    result = (
        result
        + faces[4] * (jnp.roll(inner, -1, 2) - inner)
        - faces[5] * (inner - jnp.roll(inner, 1, 2))
    )
    return result


def weighted_sum(weight_row, history):
    total = jnp.zeros(history.shape[1:], jnp.float32)
    for member in range(history.shape[0]):
        total = total + weight_row[member] * history[member]
    return total


def body(initial, mobility):
    level_count = lax.axis_size("level")
    level_id = lax.axis_index("level")
    faces = face_table(mobility)
    coefficients = jnp.asarray(quadrature_rows(STEPS), jnp.float32)
    node_ids = jnp.arange(STEPS + 1, dtype=jnp.int32)[:, None, None, None]
    solution = initial
    history = jnp.zeros((STEPS + 1,) + initial.shape, jnp.float32)
    for wave in range(STEPS + level_count - 1):
        interval = wave - level_id
        current = tendency_local(extend(solution), faces)
        arrived = passed_along(current, "level", 1)
        history = jnp.where(node_ids == interval + 1, arrived[None], history)
        weight_row = coefficients[jnp.clip(interval, 0, STEPS - 1)]
        correction = weighted_sum(weight_row, history)
        correction = jnp.where(level_id > 0, correction, jnp.zeros_like(correction))
        stepped = solution + time_step * (current + correction)
        active = jnp.logical_and(interval >= 0, interval < STEPS)
        solution = jnp.where(active, stepped, solution)
    return solution[None]


def solution(mesh):
    placed = (P("gx", "gy", None), P("gx", "gy", None))
    return jax.shard_map(
        body, mesh=mesh, in_specs=placed, out_specs=P("level", "gx", "gy", None), check_vma=False
    )
```

profile of v0, /device:TPU:1, one launch (start us, length us, event | category | flops | bytes accessed | tf_op | source)
XLA Modules:
  0.0 224.4 jit_solution(14192666357616248190)
XLA Ops:
  7.0 5.2 %collective-permute-done.1 = f32[2,32,512]{2,1,0:T(8,128)S(1)} collective-permute-done((f32[2,32,512]{2,1,0:T(8,128)S(1)}, f32[2,32,512]{2,1,0:T(8,128)S(1)}, u32[]{:S(2)}, u32[]{:S(2)}) %collective-permute-start.1) | collective-permute-done | bytes 131104 | tf_op jit(solution)/shard_map/ppermute | solution.py:20
  12.4 3.5 %collective-permute-start.4 = (f32[8,2,512]{2,1,0:T(2,128)S(1)}, f32[8,2,512]{2,1,0:T(2,128)S(1)}, u32[]{:S(2)}, u32[]{:S(2)}) collective-permute-start(f32[8,2,512]{2,1,0:T(2,128)S(1)} %get-tuple-element.56), channel_id=1, source_target_pairs={{1,0},{2,1},{3,2},{0,3},{5,4},{6,5},{7,6},{4,7},{9,8},{10,9},{11,1... | collective-permute-start | bytes 98312 | tf_op jit(solution)/shard_map/ppermute | solution.py:22
  16.0 3.3 %collective-permute-start.6 = (f32[6,1,512]{2,1,0:T(1,128)S(1)}, f32[6,1,512]{2,1,0:T(1,128)S(1)}, u32[]{:S(2)}, u32[]{:S(2)}) collective-permute-start(f32[6,1,512]{2,1,0:T(1,128)S(1)} %get-tuple-element.91), channel_id=1, source_target_pairs={{1,0},{2,1},{3,2},{0,3},{5,4},{6,5},{7,6},{4,7},{9,8},{10,9},{11,1... | collective-permute-start | bytes 36872 | tf_op jit(solution)/shard_map/ppermute | solution.py:22
  21.9 5.9 %collective-permute-start.8 = (f32[4,32,512]{2,1,0:T(8,128)S(1)}, f32[4,32,512]{2,1,0:T(8,128)S(1)}, u32[]{:S(2)}, u32[]{:S(2)}) collective-permute-start(f32[4,32,512]{2,1,0:T(8,128)S(1)} %get-tuple-element.5), channel_id=1, source_target_pairs={{0,8},{8,16},{16,24},{1,9},{9,17},{17,25},{2,10},{10,18},{18,26},{... | collective-permute-start | bytes 786440 | tf_op jit(solution)/shard_map/ppermute | solution.py:32
  31.4 4.0 %add_select_fusion.7 = f32[4,32,512]{2,1,0:T(8,128)S(1)} fusion(f32[4,32,512]{2,1,0:T(8,128)S(1)} %copy-done.3, f32[4,32,512]{2,1,0:T(8,128)S(1)} %get-tuple-element.5, f32[6,4,32,512]{3,2,1,0:T(8,128)S(1)} %broadcast_select_fusion.7, f32[]{:T(128)} %bitcast.5, f32[]{:T(128)} %bitcast.4, f32[]{:T(128)} %bitcast.3, f32[]{:T(128)} %bitcast.2, f32[]{:T(128)} %bitcast.1, ...), kind=kLoop, calls=%fused_computation.131 | loop fusion | flops 1048576 | bytes 2359322 | tf_op jit(solution)/shard_map/jit(_where)/select_n | solution.py:130
  44.1 3.5 %collective-permute-done.11 = f32[8,2,512]{2,1,0:T(2,128)S(1)} collective-permute-done((f32[8,2,512]{2,1,0:T(2,128)S(1)}, f32[8,2,512]{2,1,0:T(2,128)S(1)}, u32[]{:S(2)}, u32[]{:S(2)}) %collective-permute-start.11) | collective-permute-done | bytes 32800 | tf_op jit(solution)/shard_map/ppermute | solution.py:20
  49.0 7.0 %collective-permute-start.13 = (f32[4,32,512]{2,1,0:T(8,128)S(1)}, f32[4,32,512]{2,1,0:T(8,128)S(1)}, u32[]{:S(2)}, u32[]{:S(2)}) collective-permute-start(f32[4,32,512]{2,1,0:T(8,128)S(1)} %fusion.161), channel_id=1, source_target_pairs={{0,8},{8,16},{16,24},{1,9},{9,17},{17,25},{2,10},{10,18},{18,26},{... | collective-permute-start | bytes 786440 | tf_op jit(solution)/shard_map/ppermute | solution.py:32
  56.0 3.3 %collective-permute-done.13 = f32[4,32,512]{2,1,0:T(8,128)S(1)} collective-permute-done((f32[4,32,512]{2,1,0:T(8,128)S(1)}, f32[4,32,512]{2,1,0:T(8,128)S(1)}, u32[]{:S(2)}, u32[]{:S(2)}) %collective-permute-start.13) | collective-permute-done | bytes 262176 | tf_op jit(solution)/shard_map/ppermute | solution.py:32
  59.6 4.0 %add_select_fusion.6 = f32[4,32,512]{2,1,0:T(8,128)S(1)} fusion(f32[4,32,512]{2,1,0:T(8,128)S(1)} %add_select_fusion.7, f32[4,32,512]{2,1,0:T(8,128)S(1)} %fusion.161, f32[6,4,32,512]{3,2,1,0:T(8,128)S(1)} %broadcast_select_fusion.6, f32[]{:T(128)} %bitcast.12, f32[]{:T(128)} %bitcast.11, f32[]{:T(128)} %bitcast.10, f32[]{:T(128)} %bitcast.9, f32[]{:T(128)} %bitcast.8, ...), kind=kLoop, calls=%fused_computation.130 | loop fusion | flops 1048576 | bytes 2359322 | tf_op jit(solution)/shard_map/jit(_where)/select_n | solution.py:130
  75.1 6.6 %collective-permute-start.18 = (f32[4,32,512]{2,1,0:T(8,128)S(1)}, f32[4,32,512]{2,1,0:T(8,128)S(1)}, u32[]{:S(2)}, u32[]{:S(2)}) collective-permute-start(f32[4,32,512]{2,1,0:T(8,128)S(1)} %fusion.143), channel_id=1, source_target_pairs={{0,8},{8,16},{16,24},{1,9},{9,17},{17,25},{2,10},{10,18},{18,26},{... | collective-permute-start | bytes 786440 | tf_op jit(solution)/shard_map/ppermute | solution.py:32
  85.3 3.9 %add_select_fusion.5 = f32[4,32,512]{2,1,0:T(8,128)S(1)} fusion(f32[4,32,512]{2,1,0:T(8,128)S(1)} %add_select_fusion.6, f32[4,32,512]{2,1,0:T(8,128)S(1)} %fusion.143, f32[6,4,32,512]{3,2,1,0:T(8,128)S(1)} %broadcast_select_fusion.5, f32[]{:T(128)} %bitcast.19, f32[]{:T(128)} %bitcast.18, f32[]{:T(128)} %bitcast.17, f32[]{:T(128)} %bitcast.16, f32[]{:T(128)} %bitcast.15, ...), kind=kLoop, calls=%fused_computation.129 | loop fusion | flops 1048576 | bytes 2359322 | tf_op jit(solution)/shard_map/jit(_where)/select_n | solution.py:130
  100.9 6.4 %collective-permute-start.23 = (f32[4,32,512]{2,1,0:T(8,128)S(1)}, f32[4,32,512]{2,1,0:T(8,128)S(1)}, u32[]{:S(2)}, u32[]{:S(2)}) collective-permute-start(f32[4,32,512]{2,1,0:T(8,128)S(1)} %fusion.125), channel_id=1, source_target_pairs={{0,8},{8,16},{16,24},{1,9},{9,17},{17,25},{2,10},{10,18},{18,26},{... | collective-permute-start | bytes 786440 | tf_op jit(solution)/shard_map/ppermute | solution.py:32
  107.3 3.3 %collective-permute-done.23 = f32[4,32,512]{2,1,0:T(8,128)S(1)} collective-permute-done((f32[4,32,512]{2,1,0:T(8,128)S(1)}, f32[4,32,512]{2,1,0:T(8,128)S(1)}, u32[]{:S(2)}, u32[]{:S(2)}) %collective-permute-start.23) | collective-permute-done | bytes 262176 | tf_op jit(solution)/shard_map/ppermute | solution.py:32
  111.0 4.0 %add_select_fusion.4 = f32[4,32,512]{2,1,0:T(8,128)S(1)} fusion(f32[4,32,512]{2,1,0:T(8,128)S(1)} %add_select_fusion.5, f32[4,32,512]{2,1,0:T(8,128)S(1)} %fusion.125, f32[6,4,32,512]{3,2,1,0:T(8,128)S(1)} %broadcast_select_fusion.4, f32[]{:T(128)} %bitcast.26, f32[]{:T(128)} %bitcast.25, f32[]{:T(128)} %bitcast.24, f32[]{:T(128)} %bitcast.23, f32[]{:T(128)} %bitcast.22, ...), kind=kLoop, calls=%fused_computation.128 | loop fusion | flops 1048576 | bytes 2359322 | tf_op jit(solution)/shard_map/jit(_where)/select_n | solution.py:130
  126.7 6.6 %collective-permute-start.28 = (f32[4,32,512]{2,1,0:T(8,128)S(1)}, f32[4,32,512]{2,1,0:T(8,128)S(1)}, u32[]{:S(2)}, u32[]{:S(2)}) collective-permute-start(f32[4,32,512]{2,1,0:T(8,128)S(1)} %fusion.107), channel_id=1, source_target_pairs={{0,8},{8,16},{16,24},{1,9},{9,17},{17,25},{2,10},{10,18},{18,26},{... | collective-permute-start | bytes 786440 | tf_op jit(solution)/shard_map/ppermute | solution.py:32
  137.0 4.0 %add_select_fusion.3 = f32[4,32,512]{2,1,0:T(8,128)S(1)} fusion(f32[4,32,512]{2,1,0:T(8,128)S(1)} %add_select_fusion.4, f32[4,32,512]{2,1,0:T(8,128)S(1)} %fusion.107, f32[6,4,32,512]{3,2,1,0:T(8,128)S(1)} %broadcast_select_fusion.3, f32[]{:T(128)} %bitcast.33, f32[]{:T(128)} %bitcast.32, f32[]{:T(128)} %bitcast.31, f32[]{:T(128)} %bitcast.30, f32[]{:T(128)} %bitcast.29, ...), kind=kLoop, calls=%fused_computation.127 | loop fusion | flops 1048576 | bytes 2359322 | tf_op jit(solution)/shard_map/jit(_where)/select_n | solution.py:130
  152.7 6.4 %collective-permute-start.33 = (f32[4,32,512]{2,1,0:T(8,128)S(1)}, f32[4,32,512]{2,1,0:T(8,128)S(1)}, u32[]{:S(2)}, u32[]{:S(2)}) collective-permute-start(f32[4,32,512]{2,1,0:T(8,128)S(1)} %fusion.89), channel_id=1, source_target_pairs={{0,8},{8,16},{16,24},{1,9},{9,17},{17,25},{2,10},{10,18},{18,26},{... | collective-permute-start | bytes 786440 | tf_op jit(solution)/shard_map/ppermute | solution.py:32
  159.2 3.3 %collective-permute-done.33 = f32[4,32,512]{2,1,0:T(8,128)S(1)} collective-permute-done((f32[4,32,512]{2,1,0:T(8,128)S(1)}, f32[4,32,512]{2,1,0:T(8,128)S(1)}, u32[]{:S(2)}, u32[]{:S(2)}) %collective-permute-start.33) | collective-permute-done | bytes 262176 | tf_op jit(solution)/shard_map/ppermute | solution.py:32
  163.9 4.9 %add_select_fusion.2 = f32[4,32,512]{2,1,0:T(8,128)S(1)} fusion(f32[4,32,512]{2,1,0:T(8,128)S(1)} %add_select_fusion.3, f32[4,32,512]{2,1,0:T(8,128)} %copy-done.4, f32[6,4,32,512]{3,2,1,0:T(8,128)S(1)} %broadcast_select_fusion.2, f32[]{:T(128)} %bitcast.40, f32[]{:T(128)} %bitcast.39, f32[]{:T(128)} %bitcast.38, f32[]{:T(128)} %bitcast.37, f32[]{:T(128)} %bitcast.36, ...), kind=kLoop, calls=%fused_computation.126 | loop fusion | flops 1048576 | bytes 2359322 | tf_op jit(solution)/shard_map/jit(_where)/select_n | solution.py:130
  180.5 6.4 %collective-permute-start.38 = (f32[4,32,512]{2,1,0:T(8,128)S(1)}, f32[4,32,512]{2,1,0:T(8,128)}, u32[]{:S(2)}, u32[]{:S(2)}) collective-permute-start(f32[4,32,512]{2,1,0:T(8,128)S(1)} %fusion.71), channel_id=1, source_target_pairs={{0,8},{8,16},{16,24},{1,9},{9,17},{17,25},{2,10},{10,18},{18,26},{... | collective-permute-start | bytes 786440 | tf_op jit(solution)/shard_map/ppermute | solution.py:32
  192.1 4.0 %add_select_fusion.1 = f32[4,32,512]{2,1,0:T(8,128)S(1)} fusion(f32[4,32,512]{2,1,0:T(8,128)S(1)} %add_select_fusion.2, f32[4,32,512]{2,1,0:T(8,128)S(1)} %fusion.71, f32[6,4,32,512]{3,2,1,0:T(8,128)S(1)} %broadcast_select_fusion.1, f32[]{:T(128)} %bitcast.47, f32[]{:T(128)} %bitcast.46, f32[]{:T(128)} %bitcast.45, f32[]{:T(128)} %bitcast.44, f32[]{:T(128)} %bitcast.43, ...), kind=kLoop, calls=%fused_computation.125 | loop fusion | flops 1048576 | bytes 2359322 | tf_op jit(solution)/shard_map/jit(_where)/select_n | solution.py:130
  207.8 6.5 %collective-permute-start.43 = (f32[4,32,512]{2,1,0:T(8,128)S(1)}, f32[4,32,512]{2,1,0:T(8,128)S(1)}, u32[]{:S(2)}, u32[]{:S(2)}) collective-permute-start(f32[4,32,512]{2,1,0:T(8,128)S(1)} %fusion.53), channel_id=1, source_target_pairs={{0,8},{8,16},{16,24},{1,9},{9,17},{17,25},{2,10},{10,18},{18,26},{... | collective-permute-start | bytes 786440 | tf_op jit(solution)/shard_map/ppermute | solution.py:32
  214.3 3.3 %collective-permute-done.43 = f32[4,32,512]{2,1,0:T(8,128)S(1)} collective-permute-done((f32[4,32,512]{2,1,0:T(8,128)S(1)}, f32[4,32,512]{2,1,0:T(8,128)S(1)}, u32[]{:S(2)}, u32[]{:S(2)}) %collective-permute-start.43) | collective-permute-done | bytes 262176 | tf_op jit(solution)/shard_map/ppermute | solution.py:32
  219.7 4.7 %fusion.40 = f32[1,4,32,512]{3,2,1,0:T(8,128)} fusion(f32[4,32,512]{2,1,0:T(8,128)S(1)} %add_select_fusion.1, f32[4,32,512]{2,1,0:T(8,128)S(1)} %fusion.53, f32[6,4,32,512]{3,2,1,0:T(8,128)S(1)} %broadcast_select_fusion, f32[]{:T(128)} %bitcast.54, f32[]{:T(128)} %bitcast.53, f32[]{:T(128)} %bitcast.52, f32[]{:T(128)} %bitcast.51, f32[]{:T(128)} %bitcast.50, ...), kind=kLoop, calls=%fused_computation.132 | loop fusion | flops 1048576 | bytes 2359322 | tf_op jit(solution)/shard_map/broadcast_in_dim | solution.py:131
  (201 shorter events, 109.6 us)
Async XLA Ops:
  0.9 6.0 %collective-permute-start.5 = (f32[1,32,512]{2,1,0:T(8,128)S(1)}, f32[1,32,512]{2,1,0:T(8,128)S(1)}, u32[]{:S(2)}, u32[]{:S(2)}) collective-permute-start(f32[1,32,512]{2,1,0:T(8,128)S(1)} %get-tuple-element.110), channel_id=1, source_target_pairs={{0,4},{4,0},{1,5},{5,1},{2,6},{6,2},{3,7},{7,3},{8,12},{12,8},{9,1... | collective-permute-start | bytes 196616 | tf_op jit(solution)/shard_map/ppermute | solution.py:20
  4.1 8.2 %collective-permute-start.2 = (f32[2,32,512]{2,1,0:T(8,128)S(1)}, f32[2,32,512]{2,1,0:T(8,128)S(1)}, u32[]{:S(2)}, u32[]{:S(2)}) collective-permute-start(f32[2,32,512]{2,1,0:T(8,128)S(1)} %get-tuple-element.112), channel_id=1, source_target_pairs={{4,0},{0,4},{5,1},{1,5},{6,2},{2,6},{7,3},{3,7},{12,8},{8,12},{13,... | collective-permute-start | bytes 393224 | tf_op jit(solution)/shard_map/ppermute | solution.py:22
  5.6 6.7 %collective-permute-start.1 = (f32[2,32,512]{2,1,0:T(8,128)S(1)}, f32[2,32,512]{2,1,0:T(8,128)S(1)}, u32[]{:S(2)}, u32[]{:S(2)}) collective-permute-start(f32[2,32,512]{2,1,0:T(8,128)S(1)} %get-tuple-element.113), channel_id=1, source_target_pairs={{0,4},{4,0},{1,5},{5,1},{2,6},{6,2},{3,7},{7,3},{8,12},{12,8},{9,1... | collective-permute-start | bytes 393224 | tf_op jit(solution)/shard_map/ppermute | solution.py:20
  12.4 6.9 %collective-permute-start.4 = (f32[8,2,512]{2,1,0:T(2,128)S(1)}, f32[8,2,512]{2,1,0:T(2,128)S(1)}, u32[]{:S(2)}, u32[]{:S(2)}) collective-permute-start(f32[8,2,512]{2,1,0:T(2,128)S(1)} %get-tuple-element.56), channel_id=1, source_target_pairs={{1,0},{2,1},{3,2},{0,3},{5,4},{6,5},{7,6},{4,7},{9,8},{10,9},{11,1... | collective-permute-start | bytes 98312 | tf_op jit(solution)/shard_map/ppermute | solution.py:22
  15.9 5.6 %collective-permute-start.7 = (f32[6,1,512]{2,1,0:T(1,128)S(1)}, f32[6,1,512]{2,1,0:T(1,128)S(1)}, u32[]{:S(2)}, u32[]{:S(2)}) collective-permute-start(f32[6,1,512]{2,1,0:T(1,128)S(1)} %get-tuple-element.90), channel_id=1, source_target_pairs={{0,1},{1,2},{2,3},{3,0},{4,5},{5,6},{6,7},{7,4},{8,9},{9,10},{10,1... | collective-permute-start | bytes 36872 | tf_op jit(solution)/shard_map/ppermute | solution.py:20
  16.0 5.5 %collective-permute-start.6 = (f32[6,1,512]{2,1,0:T(1,128)S(1)}, f32[6,1,512]{2,1,0:T(1,128)S(1)}, u32[]{:S(2)}, u32[]{:S(2)}) collective-permute-start(f32[6,1,512]{2,1,0:T(1,128)S(1)} %get-tuple-element.91), channel_id=1, source_target_pairs={{1,0},{2,1},{3,2},{0,3},{5,4},{6,5},{7,6},{4,7},{9,8},{10,9},{11,1... | collective-permute-start | bytes 36872 | tf_op jit(solution)/shard_map/ppermute | solution.py:22
  21.9 9.2 %collective-permute-start.8 = (f32[4,32,512]{2,1,0:T(8,128)S(1)}, f32[4,32,512]{2,1,0:T(8,128)S(1)}, u32[]{:S(2)}, u32[]{:S(2)}) collective-permute-start(f32[4,32,512]{2,1,0:T(8,128)S(1)} %get-tuple-element.5), channel_id=1, source_target_pairs={{0,8},{8,16},{16,24},{1,9},{9,17},{17,25},{2,10},{10,18},{18,26},{... | collective-permute-start | bytes 786440 | tf_op jit(solution)/shard_map/ppermute | solution.py:32
  49.0 10.3 %collective-permute-start.13 = (f32[4,32,512]{2,1,0:T(8,128)S(1)}, f32[4,32,512]{2,1,0:T(8,128)S(1)}, u32[]{:S(2)}, u32[]{:S(2)}) collective-permute-start(f32[4,32,512]{2,1,0:T(8,128)S(1)} %fusion.161), channel_id=1, source_target_pairs={{0,8},{8,16},{16,24},{1,9},{9,17},{17,25},{2,10},{10,18},{18,26},{... | collective-permute-start | bytes 786440 | tf_op jit(solution)/shard_map/ppermute | solution.py:32
  69.1 4.6 %collective-permute-start.16 = (f32[8,2,512]{2,1,0:T(2,128)S(1)}, f32[8,2,512]{2,1,0:T(2,128)S(1)}, u32[]{:S(2)}, u32[]{:S(2)}) collective-permute-start(f32[8,2,512]{2,1,0:T(2,128)S(1)} %get-tuple-element.53), channel_id=1, source_target_pairs={{0,1},{1,2},{2,3},{3,0},{4,5},{5,6},{6,7},{7,4},{8,9},{9,10},{10,1... | collective-permute-start | bytes 98312 | tf_op jit(solution)/shard_map/ppermute | solution.py:20
  75.1 9.9 %collective-permute-start.18 = (f32[4,32,512]{2,1,0:T(8,128)S(1)}, f32[4,32,512]{2,1,0:T(8,128)S(1)}, u32[]{:S(2)}, u32[]{:S(2)}) collective-permute-start(f32[4,32,512]{2,1,0:T(8,128)S(1)} %fusion.143), channel_id=1, source_target_pairs={{0,8},{8,16},{16,24},{1,9},{9,17},{17,25},{2,10},{10,18},{18,26},{... | collective-permute-start | bytes 786440 | tf_op jit(solution)/shard_map/ppermute | solution.py:32
  90.1 4.7 %collective-permute-start.20 = (f32[2,32,512]{2,1,0:T(8,128)S(1)}, f32[2,32,512]{2,1,0:T(8,128)S(1)}, u32[]{:S(2)}, u32[]{:S(2)}) collective-permute-start(f32[2,32,512]{2,1,0:T(8,128)S(1)} %get-tuple-element.101), channel_id=1, source_target_pairs={{4,0},{0,4},{5,1},{1,5},{6,2},{2,6},{7,3},{3,7},{12,8},{8,12},{13,... | collective-permute-start | bytes 393224 | tf_op jit(solution)/shard_map/ppermute | solution.py:22
  94.9 4.6 %collective-permute-start.21 = (f32[8,2,512]{2,1,0:T(2,128)S(1)}, f32[8,2,512]{2,1,0:T(2,128)S(1)}, u32[]{:S(2)}, u32[]{:S(2)}) collective-permute-start(f32[8,2,512]{2,1,0:T(2,128)S(1)} %get-tuple-element.51), channel_id=1, source_target_pairs={{0,1},{1,2},{2,3},{3,0},{4,5},{5,6},{6,7},{7,4},{8,9},{9,10},{10,1... | collective-permute-start | bytes 98312 | tf_op jit(solution)/shard_map/ppermute | solution.py:20
  100.9 9.7 %collective-permute-start.23 = (f32[4,32,512]{2,1,0:T(8,128)S(1)}, f32[4,32,512]{2,1,0:T(8,128)S(1)}, u32[]{:S(2)}, u32[]{:S(2)}) collective-permute-start(f32[4,32,512]{2,1,0:T(8,128)S(1)} %fusion.125), channel_id=1, source_target_pairs={{0,8},{8,16},{16,24},{1,9},{9,17},{17,25},{2,10},{10,18},{18,26},{... | collective-permute-start | bytes 786440 | tf_op jit(solution)/shard_map/ppermute | solution.py:32
  115.9 4.7 %collective-permute-start.25 = (f32[2,32,512]{2,1,0:T(8,128)S(1)}, f32[2,32,512]{2,1,0:T(8,128)S(1)}, u32[]{:S(2)}, u32[]{:S(2)}) collective-permute-start(f32[2,32,512]{2,1,0:T(8,128)S(1)} %get-tuple-element.99), channel_id=1, source_target_pairs={{4,0},{0,4},{5,1},{1,5},{6,2},{2,6},{7,3},{3,7},{12,8},{8,12},{13,... | collective-permute-start | bytes 393224 | tf_op jit(solution)/shard_map/ppermute | solution.py:22
  120.7 4.6 %collective-permute-start.26 = (f32[8,2,512]{2,1,0:T(2,128)S(1)}, f32[8,2,512]{2,1,0:T(2,128)S(1)}, u32[]{:S(2)}, u32[]{:S(2)}) collective-permute-start(f32[8,2,512]{2,1,0:T(2,128)S(1)} %get-tuple-element.49), channel_id=1, source_target_pairs={{0,1},{1,2},{2,3},{3,0},{4,5},{5,6},{6,7},{7,4},{8,9},{9,10},{10,1... | collective-permute-start | bytes 98312 | tf_op jit(solution)/shard_map/ppermute | solution.py:20
  126.7 9.7 %collective-permute-start.28 = (f32[4,32,512]{2,1,0:T(8,128)S(1)}, f32[4,32,512]{2,1,0:T(8,128)S(1)}, u32[]{:S(2)}, u32[]{:S(2)}) collective-permute-start(f32[4,32,512]{2,1,0:T(8,128)S(1)} %fusion.107), channel_id=1, source_target_pairs={{0,8},{8,16},{16,24},{1,9},{9,17},{17,25},{2,10},{10,18},{18,26},{... | collective-permute-start | bytes 786440 | tf_op jit(solution)/shard_map/ppermute | solution.py:32
  141.9 4.7 %collective-permute-start.30 = (f32[2,32,512]{2,1,0:T(8,128)S(1)}, f32[2,32,512]{2,1,0:T(8,128)S(1)}, u32[]{:S(2)}, u32[]{:S(2)}) collective-permute-start(f32[2,32,512]{2,1,0:T(8,128)S(1)} %get-tuple-element.97), channel_id=1, source_target_pairs={{4,0},{0,4},{5,1},{1,5},{6,2},{2,6},{7,3},{3,7},{12,8},{8,12},{13,... | collective-permute-start | bytes 393224 | tf_op jit(solution)/shard_map/ppermute | solution.py:22
  146.7 4.6 %collective-permute-start.31 = (f32[8,2,512]{2,1,0:T(2,128)S(1)}, f32[8,2,512]{2,1,0:T(2,128)S(1)}, u32[]{:S(2)}, u32[]{:S(2)}) collective-permute-start(f32[8,2,512]{2,1,0:T(2,128)S(1)} %get-tuple-element.47), channel_id=1, source_target_pairs={{0,1},{1,2},{2,3},{3,0},{4,5},{5,6},{6,7},{7,4},{8,9},{9,10},{10,1... | collective-permute-start | bytes 98312 | tf_op jit(solution)/shard_map/ppermute | solution.py:20
  152.7 9.7 %collective-permute-start.33 = (f32[4,32,512]{2,1,0:T(8,128)S(1)}, f32[4,32,512]{2,1,0:T(8,128)S(1)}, u32[]{:S(2)}, u32[]{:S(2)}) collective-permute-start(f32[4,32,512]{2,1,0:T(8,128)S(1)} %fusion.89), channel_id=1, source_target_pairs={{0,8},{8,16},{16,24},{1,9},{9,17},{17,25},{2,10},{10,18},{18,26},{... | collective-permute-start | bytes 786440 | tf_op jit(solution)/shard_map/ppermute | solution.py:32
  169.7 4.7 %collective-permute-start.35 = (f32[2,32,512]{2,1,0:T(8,128)S(1)}, f32[2,32,512]{2,1,0:T(8,128)S(1)}, u32[]{:S(2)}, u32[]{:S(2)}) collective-permute-start(f32[2,32,512]{2,1,0:T(8,128)S(1)} %get-tuple-element.95), channel_id=1, source_target_pairs={{4,0},{0,4},{5,1},{1,5},{6,2},{2,6},{7,3},{3,7},{12,8},{8,12},{13,... | collective-permute-start | bytes 393224 | tf_op jit(solution)/shard_map/ppermute | solution.py:22
  174.5 4.6 %collective-permute-start.36 = (f32[8,2,512]{2,1,0:T(2,128)S(1)}, f32[8,2,512]{2,1,0:T(2,128)S(1)}, u32[]{:S(2)}, u32[]{:S(2)}) collective-permute-start(f32[8,2,512]{2,1,0:T(2,128)S(1)} %get-tuple-element.45), channel_id=1, source_target_pairs={{0,1},{1,2},{2,3},{3,0},{4,5},{5,6},{6,7},{7,4},{8,9},{9,10},{10,1... | collective-permute-start | bytes 98312 | tf_op jit(solution)/shard_map/ppermute | solution.py:20
  180.5 9.7 %collective-permute-start.38 = (f32[4,32,512]{2,1,0:T(8,128)S(1)}, f32[4,32,512]{2,1,0:T(8,128)}, u32[]{:S(2)}, u32[]{:S(2)}) collective-permute-start(f32[4,32,512]{2,1,0:T(8,128)S(1)} %fusion.71), channel_id=1, source_target_pairs={{0,8},{8,16},{16,24},{1,9},{9,17},{17,25},{2,10},{10,18},{18,26},{... | collective-permute-start | bytes 786440 | tf_op jit(solution)/shard_map/ppermute | solution.py:32
  196.9 4.7 %collective-permute-start.40 = (f32[2,32,512]{2,1,0:T(8,128)S(1)}, f32[2,32,512]{2,1,0:T(8,128)S(1)}, u32[]{:S(2)}, u32[]{:S(2)}) collective-permute-start(f32[2,32,512]{2,1,0:T(8,128)S(1)} %get-tuple-element.93), channel_id=1, source_target_pairs={{4,0},{0,4},{5,1},{1,5},{6,2},{2,6},{7,3},{3,7},{12,8},{8,12},{13,... | collective-permute-start | bytes 393224 | tf_op jit(solution)/shard_map/ppermute | solution.py:22
  207.8 9.8 %collective-permute-start.43 = (f32[4,32,512]{2,1,0:T(8,128)S(1)}, f32[4,32,512]{2,1,0:T(8,128)S(1)}, u32[]{:S(2)}, u32[]{:S(2)}) collective-permute-start(f32[4,32,512]{2,1,0:T(8,128)S(1)} %fusion.53), channel_id=1, source_target_pairs={{0,8},{8,16},{16,24},{1,9},{9,17},{17,25},{2,10},{10,18},{18,26},{... | collective-permute-start | bytes 786440 | tf_op jit(solution)/shard_map/ppermute | solution.py:32
  (33 other events, 266.7 us)
where the time goes:
time: 225 us; the launch traced here: 224 us
  starting transfers between devices  84.5 us (38%)
  waiting for transfers between devices  81 us (36%)
  other arithmetic  47.3 us (21%)
  local copies, waits for them, and re-layouts  10.7 us (5%)
    ppermute x8, starting transfers between devices, passed_along(): return lax.ppermute(shard, axis, pairs)  51.6 us
    ppermute x18, waiting for transfers between devices, padded_2(): lax.ppermute(tail, axis, [(i, (i + 1) % count) for i in range(count)])  38 us
    select_n x7, other arithmetic, body(): solution = jnp.where(active, stepped, solution)  28.8 us
    ppermute x8, waiting for transfers between devices, passed_along(): return lax.ppermute(shard, axis, pairs)  23.2 us
    ppermute x18, waiting for transfers between devices, padded_2(): lax.ppermute(head, axis, [((i + 1) % count, i) for i in range(count)])  19.9 us
    ppermute x18, starting transfers between devices, padded_2(): lax.ppermute(tail, axis, [(i, (i + 1) % count) for i in range(count)])  17.1 us
    ppermute x18, starting transfers between devices, padded_2(): lax.ppermute(head, axis, [((i + 1) % count, i) for i in range(count)])  15.7 us
    select_n x8, other arithmetic, body(): history = jnp.where(node_ids == interval + 1, arrived[None], history)  7.19 us
  transfers between devices with their start and end apart: 44, of which 38 were waited for; matrix products, arithmetic and copies ran while one was open for 3% of the time, Pallas kernels for 0%

commit v1 on v0

--- a/solution.py
+++ b/solution.py
@@ -1,6 +1,10 @@
+import functools
+
 import jax
 import jax.numpy as jnp
 from jax import lax
+from jax.experimental import pallas as pl
+from jax.experimental.pallas import tpu as pltpu
 from jax.sharding import PartitionSpec as P
 
 STEPS = 5
@@ -131,8 +135,316 @@
     return solution[None]
 
 
+def window_kernel(weights, c_ref, m_ref, out_ref, raw, c0, mx, my, mz, rates_a, rates_b, sol_a, sol_b,
+                  ready, finals, send_sem, recv_sem, fwd_send_sem, fwd_recv_sem, own_sem,
+                  fin_send_sem, fin_recv_sem, fin_own_sem):
+    steps = len(weights)
+    level = lax.axis_index("level")
+    gx = lax.axis_index("gx")
+    gy = lax.axis_index("gy")
+    count_y = lax.axis_size("gy")
+    x = level // 2
+    core = level % 2
+    tile = 2 * gx + x
+    above = lax.rem(gy + 1, count_y)
+    below = lax.rem(gy + count_y - 1, count_y)
+    mesh_type = pl.DeviceIdType.MESH
+
+    barrier = pltpu.get_barrier_semaphore()
+    greeted = [(level + 1 - 2 * core, gx, gy)]
+    greeted += [(2 * (1 - x) + core, gx, gy), (2 * (1 - x) + core, 1 - gx, gy), (level, 1 - gx, gy)]
+    greeted += [(level, side, other) for side in (gx, 1 - gx) for other in (above, below)]
+    for device in greeted:
+        pl.semaphore_signal(barrier, inc=1, device_id=device, device_id_type=mesh_type)
+    pl.semaphore_wait(barrier, len(greeted))
+
+    def aligned(row):
+        return pl.multiple_of(row, 8)
+
+    def region(array, half, row, count):
+        return raw.at[array, pl.ds(4 * half, 4), pl.ds(aligned(row), count), :]
+
+    def outgoing(array, source):
+        partner_tile = 2 * (1 - gx) + x
+        low = jnp.where(partner_tile == 3, 1, 0)
+
+        def piece(row, count):
+            return source.at[:, pl.ds(aligned(row), count), :]
+
+        def copy(src, dst, slot, kind, device):
+            return pltpu.make_async_remote_copy(
+                src_ref=src, dst_ref=dst, send_sem=send_sem.at[slot], recv_sem=recv_sem.at[kind],
+                device_id=device, device_id_type=mesh_type)
+
+        to_above = (level, 0, above)
+        to_below = (level, 1, below)
+        partner = (level, 1 - gx, gy)
+        row_to = 8 * jnp.maximum(2 - partner_tile, 0)
+        return [
+            (None, copy(piece(8 * low, 24), region(array, gx, row_to, 24), 0, 0, partner)),
+            (x == gx, copy(piece(24, 8), region(array, gx, jnp.where(x == gx, 8 * (5 - partner_tile), 0), 8), 1, 1, partner)),
+            (x == 0, copy(piece(16, 16), region(array, gx, 0, 16), 2, 2 + gx, to_above)),
+            (x == 1, copy(piece(24, 8), region(array, gx, 0, 8), 2, 2 + gx, to_above)),
+            (x == 1, copy(piece(0, 16), region(array, gx, 24, 16), 3, 3 - gx, to_below)),
+            (x == 0, copy(piece(0, 8), region(array, gx, 32, 8), 3, 3 - gx, to_below)),
+        ]
+
+    def when(condition, action):
+        if condition is None:
+            action()
+        else:
+            pl.when(condition)(action)
+
+    sibling = (level + 1 - 2 * core, gx, gy)
+
+    def arriving(array):
+        def copy(half, row, count, kind):
+            where = region(array, half, row, count)
+            landed = pltpu.make_async_remote_copy(
+                src_ref=where, dst_ref=where, send_sem=send_sem.at[0], recv_sem=recv_sem.at[kind],
+                device_id=sibling, device_id_type=mesh_type)
+            handed = pltpu.make_async_remote_copy(
+                src_ref=where, dst_ref=where, send_sem=fwd_send_sem.at[kind],
+                recv_sem=fwd_recv_sem.at[kind], device_id=sibling, device_id_type=mesh_type)
+            return landed, handed
+
+        same = x == gx
+        entries = [
+            (None, copy(1 - gx, 8 * jnp.maximum(2 - tile, 0), 24, 0)),
+            (jnp.logical_not(same), copy(1 - gx, jnp.where(same, 0, 8 * (5 - tile)), 8, 1)),
+        ]
+        for half, kind in ((gx, 2), (1 - gx, 3)):
+            entries.append((same, copy(half, 24 * gx, 16, kind)))
+            entries.append((jnp.logical_not(same), copy(half, 32 * gx, 8, kind)))
+        return entries
+
+    def own(array, source):
+        low = jnp.where(tile == 3, 1, 0)
+        row_to = 8 * jnp.maximum(2 - tile, 0)
+        return [
+            (None, pltpu.make_async_copy(
+                source.at[:, pl.ds(aligned(8 * low), 24), :], region(array, gx, row_to, 24), own_sem.at[array, 0])),
+            (x != gx, pltpu.make_async_copy(
+                source.at[:, pl.ds(24, 8), :], region(array, gx, jnp.where(x != gx, 8 * (5 - tile), 0), 8),
+                own_sem.at[array, 1])),
+        ]
+
+    for array, source in enumerate((c_ref, m_ref)):
+        @pl.when(core == array)
+        def _(array=array, source=source):
+            for condition, copy in outgoing(array, source):
+                when(condition, copy.start)
+    for array, source in enumerate((c_ref, m_ref)):
+        for condition, copy in own(array, source):
+            when(condition, copy.start)
+    for array in range(2):
+        @pl.when(core == array)
+        def _(array=array):
+            for condition, (landed, handed) in arriving(array):
+                def pass_on(landed=landed, handed=handed):
+                    landed.wait_recv()
+                    handed.start()
+                when(condition, pass_on)
+    for array, source in enumerate((c_ref, m_ref)):
+        for condition, copy in own(array, source):
+            when(condition, copy.wait)
+    for array, source in enumerate((c_ref, m_ref)):
+        @pl.when(core == array)
+        def _(array=array, source=source):
+            for condition, copy in outgoing(array, source):
+                when(condition, copy.wait_send)
+            for condition, (landed, handed) in arriving(array):
+                when(condition, handed.wait_send)
+            for condition, (landed, handed) in arriving(1 - array):
+                when(condition, handed.wait_recv)
+
+    width = c_ref.shape[2]
+
+    def roll_x(cells, by):
+        return pltpu.roll(cells, by % 8, 0)
+
+    def roll_z(cells, by):
+        return pltpu.roll(cells, by % width, 1)
+
+    def turn(block, carry):
+        row = pl.multiple_of(8 * block, 8)
+        for array, target in ((0, c0), (1, sol_a)):
+            for lane in range(0, width, 128):
+                cells = raw[array, :, pl.ds(row, 8), lane:lane + 128]
+                target[pl.ds(row, 8), :, lane:lane + 128] = jnp.swapaxes(cells, 0, 1)
+        return carry
+
+    lax.fori_loop(0, 5, turn, 0)
+
+    half_step = 0.5 * time_step
+
+    def faces(row, carry):
+        here = sol_a[row]
+        mx[row] = half_step * (here + roll_x(here, -1))
+        mz[row] = half_step * (here + roll_z(here, -1))
+        my[row] = half_step * (here + sol_a[row + 1])
+        return carry
+
+    lax.fori_loop(1, 39, faces, 0)
+
+    def potential(state, row):
+        centre = state[row]
+        around = state[row - 1] + state[row + 1]
+        around = around + (roll_x(centre, 1) + roll_x(centre, -1))
+        around = around + (roll_z(centre, 1) + roll_z(centre, -1))
+        return (centre * centre + (6.0 * gradient_energy - 1.0)) * centre - gradient_energy * around
+
+    def evaluate(state, reach, rates_out, update):
+        first, last = 16 - reach, 24 + reach
+        here = potential(state, first)
+        flux = my[first - 1] * (here - potential(state, first - 1))
+
+        def group(index, carry):
+            here, flux = carry
+            for offset in range(4):
+                row = first + 4 * index + offset
+                after = potential(state, row + 1)
+                flux_after = my[row] * (after - here)
+                flux_x = mx[row] * (roll_x(here, -1) - here)
+                flux_z = mz[row] * (roll_z(here, -1) - here)
+                rate = flux_after - flux
+                rate = rate + (flux_x - roll_x(flux_x, 1))
+                rate = rate + (flux_z - roll_z(flux_z, 1))
+                if rates_out is not None:
+                    rates_out[row] = rate
+                if update is not None:
+                    update(row, rate)
+                here, flux = after, flux_after
+            return here, flux
+
+        lax.fori_loop(0, (last - first) // 4, group, (here, flux))
+
+    def deliveries(slot):
+        result = []
+        into = finals.at[:, pl.ds(aligned(8 * tile), 8), :]
+        for to_x, to_gx in ((slot, 0), (slot, 1)):
+            stays = jnp.logical_and(x == to_x, gx == to_gx)
+            out = ready.at[slot, pl.ds(4 * to_gx, 4)]
+            remote = pltpu.make_async_remote_copy(
+                src_ref=out, dst_ref=into, send_sem=fin_send_sem.at[2 * slot + to_gx],
+                recv_sem=fin_recv_sem.at[tile], device_id=(2 * to_x + core, to_gx, gy),
+                device_id_type=mesh_type)
+            local = pltpu.make_async_copy(out, into, fin_own_sem)
+            result.append((pl.when(jnp.logical_not(stays)), remote, pl.when(stays), local))
+        return result
+
+    def send_out(slot, state):
+        for lane in range(0, width, 128):
+            ready[slot, :, :, lane:lane + 128] = jnp.swapaxes(state[16:24, :, lane:lane + 128], 0, 1)
+        for goes, remote, stays, local in deliveries(slot):
+            goes(remote.start)
+            stays(local.start)
+
+    first_reach = 2 * (steps + 2)
+
+    def run_level(index):
+        below_rates = (rates_a, rates_b)[(index + 1) % 2]
+        own_rates = (rates_a, rates_b)[index % 2]
+        states = (sol_a, sol_b)
+
+        def below_rate(node, row):
+            return rates_a[0, row] if node == 0 else below_rates[node, row]
+
+        def corrected(interval, row, base, rate):
+            total = rate
+            if index > 0:
+                for node in range(interval + 2):
+                    factor = weights[interval][node]
+                    if interval == 0 and node == 0:
+                        factor = factor + 1.0
+                        total = factor * below_rate(0, row)
+                    else:
+                        total = total + factor * below_rate(node, row)
+            return base + total
+
+        for interval in range(steps + 1):
+            reach = first_reach - 2 * (index + interval)
+            source = c0 if interval == 0 else states[interval % 2]
+            target = states[(interval + 1) % 2]
+
+            def update(row, rate, interval=interval, source=source, target=target):
+                target[row] = corrected(interval, row, source[row], rate)
+
+            if interval == 0 and index > 0:
+                def start(group, carry, update=update, reach=reach):
+                    for offset in range(4):
+                        update(16 - reach + 4 * group + offset, None)
+                    return carry
+                lax.fori_loop(0, (8 + 2 * reach) // 4, start, 0)
+            elif interval < steps:
+                evaluate(source, reach, own_rates.at[interval] if index < 3 else None, update)
+            elif index < 3:
+                evaluate(source, reach, own_rates.at[interval], None)
+            if interval == steps - 1:
+                @pl.when(core == index % 2)
+                def _(target=target):
+                    send_out(index // 2, target)
+
+    for index in range(3):
+        run_level(index)
+    pl.when(core == 1)(lambda: run_level(3))
+
+    for slot in range(2):
+        for goes, remote, stays, local in deliveries(slot):
+            goes(remote.wait_send)
+            stays(local.wait)
+    for source_tile in range(4):
+        into = finals.at[:, pl.ds(8 * source_tile, 8), :]
+        arrived = pltpu.make_async_remote_copy(
+            src_ref=into, dst_ref=into, send_sem=fin_send_sem.at[0],
+            recv_sem=fin_recv_sem.at[source_tile], device_id=sibling, device_id_type=mesh_type)
+        pl.when(tile != source_tile)(arrived.wait_recv)
+    out_ref[0] = finals[...]
+
+
+def window_body(initial, mobility):
+    f32 = jnp.float32
+    width = initial.shape[2]
+    weights = quadrature_rows(STEPS)
+    field = pltpu.VMEM((40, 8, width), f32)
+    return pl.pallas_call(
+        functools.partial(window_kernel, weights),
+        out_shape=jax.ShapeDtypeStruct((1,) + initial.shape, f32),
+        in_specs=[pl.BlockSpec(memory_space=pltpu.VMEM)] * 2,
+        out_specs=pl.BlockSpec(memory_space=pltpu.VMEM),
+        scratch_shapes=[
+            pltpu.VMEM((2, 8, 40, width), f32),
+            field, field, field, field,
+            pltpu.VMEM((STEPS + 1, 40, 8, width), f32),
+            pltpu.VMEM((STEPS + 1, 40, 8, width), f32),
+            field, field,
+            pltpu.VMEM((2, 8, 8, width), f32),
+            pltpu.VMEM(initial.shape, f32),
+            pltpu.SemaphoreType.DMA((4,)),
+            pltpu.SemaphoreType.DMA((4,)),
+            pltpu.SemaphoreType.DMA((4,)),
+            pltpu.SemaphoreType.DMA((4,)),
+            pltpu.SemaphoreType.DMA((2, 2)),
+            pltpu.SemaphoreType.DMA((4,)),
+            pltpu.SemaphoreType.DMA((4,)),
+            pltpu.SemaphoreType.DMA,
+        ],
+        compiler_params=pltpu.CompilerParams(
+            collective_id=0, has_side_effects=True, vmem_limit_bytes=40 * 1024 * 1024
+        ),
+    )(initial, mobility)
+
+
 def solution(mesh):
     placed = (P("gx", "gy", None), P("gx", "gy", None))
+
+    def chosen(initial, mobility):
+        sizes = mesh.shape
+        whole = (sizes["level"], sizes["gx"]) == (4, 2) and initial.shape[:2] == (4, 32)
+        if whole and sizes["gy"] > 1 and initial.shape[2] % 128 == 0:
+            return window_body(initial, mobility)
+        return body(initial, mobility)
+
     return jax.shard_map(
-        body, mesh=mesh, in_specs=placed, out_specs=P("level", "gx", "gy", None), check_vma=False
+        chosen, mesh=mesh, in_specs=placed, out_specs=P("level", "gx", "gy", None), check_vma=False
     )

time: 225 us -> 49.4 us (0.22)
  starting transfers between devices: 84.5 us -> 0 us
  waiting for transfers between devices: 81 us -> 0 us
  other arithmetic: 47.3 us -> 0 us
  Pallas kernels: 0 us -> 46.6 us
  local copies, waits for them, and re-layouts: 10.7 us -> 2.6 us
    ppermute x44 -> x0, starting transfers between devices: 84.5 us -> none  [the longest x8 51.6 us: passed_along(): return lax.ppermute(shard, axis, pairs)]
    ppermute x44 -> x0, waiting for transfers between devices: 81 us -> none  [the longest x18 38 us: padded_2(): lax.ppermute(tail, axis, [(i, (i + 1) % count) for i in range(count)])]
    pallas_call x0 -> x1, Pallas kernels: none -> 46.6 us  [window_body(): pl.pallas_call(functools.partial(window_kernel, weights), out_shape=jax.S...]
    select_n x15 -> x0, other arithmetic: 36 us -> none  [the longest x7 28.8 us: body(): solution = jnp.where(active, stepped, solution)]
    slice x49 -> x0, local copies, waits for them, and re-layouts: 10.5 us -> none  [the longest x4 2.76 us: weighted_sum(): total = total + weight_row[member] * history[member]]
    sub x16 -> x0, other arithmetic: 5.61 us -> none  [the longest x8 2.96 us: tendency_local(): potential = centre * centre * centre - centre - gradient_energy * laplace]
    broadcast_in_dim x1 -> x0, other arithmetic: 4.75 us -> none  [body(): return solution[None]]
    unnamed x30 -> x5, local copies, waits for them, and re-layouts: 0.11 us -> 2.6 us
  transfers between devices with their start and end apart: 44 -> 0, of which waited for: 38 -> 0; matrix products, arithmetic and copies ran while one was open for 3% -> 0% of each run, Pallas kernels for 0% -> 0%
where the time goes in v1:
time: 49.4 us; the launch traced here: 49.3 us
  Pallas kernels  46.6 us (94%)
  local copies, waits for them, and re-layouts  2.6 us (5%)
    pallas_call x1, Pallas kernels, window_body(): pl.pallas_call(functools.partial(window_kernel, weights), out_shape=jax.S...  46.6 us
    unnamed x5, local copies, waits for them, and re-layouts  2.6 us

profile of v1, /device:TPU:1, one launch (start us, length us, event | category | flops | bytes accessed | tf_op | source)
XLA Modules:
  0.0 49.3 jit_solution(3513948915405979778)
XLA Ops:
  0.0 0.0 copy-start
  0.0 0.9 %copy-done = f32[4,32,512]{2,1,0:T(8,128)S(1)} copy-done((f32[4,32,512]{2,1,0:T(8,128)S(1)}, f32[4,32,512]{2,1,0:T(8,128)}, u32[]{:S(2)}) %copy-start) | copy-done | bytes 262168
  1.0 0.0 copy-start.1
  1.0 0.9 %copy-done.1 = f32[4,32,512]{2,1,0:T(8,128)S(1)} copy-done((f32[4,32,512]{2,1,0:T(8,128)S(1)}, f32[4,32,512]{2,1,0:T(8,128)}, u32[]{:S(2)}) %copy-start.1) | copy-done | bytes 262168
  1.9 46.6 %shard_map.28 = f32[1,4,32,512]{3,2,1,0:T(8,128)S(1)} custom-call(f32[4,32,512]{2,1,0:T(8,128)S(1)} %copy-done, f32[4,32,512]{2,1,0:T(8,128)S(1)} %copy-done.1), custom_call_target="tpu_custom_call" | custom-call | tf_op jit(solution)/shard_map/pallas_call | solution.py:410
  48.5 0.7 %copy.4 = f32[1,4,32,512]{3,2,1,0:T(8,128)} copy(f32[1,4,32,512]{3,2,1,0:T(8,128)S(1)} %shard_map.28) | data formatting | bytes 524288
Async XLA Ops:
  0.0 0.9 %copy-start = (f32[4,32,512]{2,1,0:T(8,128)S(1)}, f32[4,32,512]{2,1,0:T(8,128)}, u32[]{:S(2)}) copy-start(f32[4,32,512]{2,1,0:T(8,128)} %c_ref.1) | copy-start | bytes 786436
  1.0 0.9 %copy-start.1 = (f32[4,32,512]{2,1,0:T(8,128)S(1)}, f32[4,32,512]{2,1,0:T(8,128)}, u32[]{:S(2)}) copy-start(f32[4,32,512]{2,1,0:T(8,128)} %m_ref.1) | copy-start | bytes 786436

commit v2 on v1

--- a/solution.py
+++ b/solution.py
@@ -136,7 +136,7 @@
 
 
 def window_kernel(weights, c_ref, m_ref, out_ref, raw, c0, mx, my, mz, rates_a, rates_b, sol_a, sol_b,
-                  ready, finals, send_sem, recv_sem, fwd_send_sem, fwd_recv_sem, own_sem,
+                  ready, finals, stage, send_sem, recv_sem, fwd_send_sem, fwd_recv_sem, own_sem,
                   fin_send_sem, fin_recv_sem, fin_own_sem):
     steps = len(weights)
     level = lax.axis_index("level")
@@ -156,8 +156,6 @@
     greeted += [(level, side, other) for side in (gx, 1 - gx) for other in (above, below)]
     for device in greeted:
         pl.semaphore_signal(barrier, inc=1, device_id=device, device_id_type=mesh_type)
-    pl.semaphore_wait(barrier, len(greeted))
-
     def aligned(row):
         return pl.multiple_of(row, 8)
 
@@ -229,12 +227,40 @@
                 own_sem.at[array, 1])),
         ]
 
+    width = c_ref.shape[2]
+    parts = width // 128
+
+    def one_hot(inverse):
+        natural = lax.broadcasted_iota(jnp.int32, (width, width), 1 if inverse else 0)
+        placed = lax.broadcasted_iota(jnp.int32, (width, width), 0 if inverse else 1)
+        hit = natural == parts * lax.rem(placed, 128) + placed // 128
+        return jnp.where(hit, 1.0, 0.0).astype(jnp.bfloat16)
+
+    def moved(cells, matrix):
+        high = cells.astype(jnp.bfloat16)
+        rest = cells - high.astype(jnp.float32)
+        middle = rest.astype(jnp.bfloat16)
+        low = (rest - middle.astype(jnp.float32)).astype(jnp.bfloat16)
+        taken = [jnp.dot(part, matrix, preferred_element_type=jnp.float32) for part in (high, middle, low)]
+        return (taken[0] + taken[1]) + taken[2]
+
+    def interleave(array, source):
+        matrix = one_hot(False)
+        for layer in range(4):
+            stage[array, layer] = moved(source[layer], matrix)
+
     for array, source in enumerate((c_ref, m_ref)):
+        pl.when(core == array)(functools.partial(interleave, array, source))
+    pl.semaphore_wait(barrier, len(greeted))
+    for array in range(2):
         @pl.when(core == array)
-        def _(array=array, source=source):
-            for condition, copy in outgoing(array, source):
+        def _(array=array):
+            for condition, copy in outgoing(array, stage.at[array]):
                 when(condition, copy.start)
     for array, source in enumerate((c_ref, m_ref)):
+        pl.when(core != array)(functools.partial(interleave, array, source))
+    staged = (stage.at[0], stage.at[1])
+    for array, source in enumerate(staged):
         for condition, copy in own(array, source):
             when(condition, copy.start)
     for array in range(2):
@@ -245,10 +271,10 @@
                     landed.wait_recv()
                     handed.start()
                 when(condition, pass_on)
-    for array, source in enumerate((c_ref, m_ref)):
+    for array, source in enumerate(staged):
         for condition, copy in own(array, source):
             when(condition, copy.wait)
-    for array, source in enumerate((c_ref, m_ref)):
+    for array, source in enumerate(staged):
         @pl.when(core == array)
         def _(array=array, source=source):
             for condition, copy in outgoing(array, source):
@@ -258,13 +284,16 @@
             for condition, (landed, handed) in arriving(1 - array):
                 when(condition, handed.wait_recv)
 
-    width = c_ref.shape[2]
-
     def roll_x(cells, by):
         return pltpu.roll(cells, by % 8, 0)
 
     def roll_z(cells, by):
-        return pltpu.roll(cells, by % width, 1)
+        pieces = [cells[:, 128 * part:128 * part + 128] for part in range(parts)]
+        if by < 0:
+            pieces = pieces[1:] + [pltpu.roll(pieces[0], 127, 1)]
+        else:
+            pieces = [pltpu.roll(pieces[-1], 1, 1)] + pieces[:-1]
+        return jnp.concatenate(pieces, axis=1)
 
     def turn(block, carry):
         row = pl.multiple_of(8 * block, 8)
@@ -296,13 +325,14 @@
 
     def evaluate(state, reach, rates_out, update):
         first, last = 16 - reach, 24 + reach
+        size = max(count for count in range(4, 17) if (last - first) % count == 0)
         here = potential(state, first)
         flux = my[first - 1] * (here - potential(state, first - 1))
 
         def group(index, carry):
             here, flux = carry
-            for offset in range(4):
-                row = first + 4 * index + offset
+            for offset in range(size):
+                row = first + size * index + offset
                 after = potential(state, row + 1)
                 flux_after = my[row] * (after - here)
                 flux_x = mx[row] * (roll_x(here, -1) - here)
@@ -317,7 +347,7 @@
                 here, flux = after, flux_after
             return here, flux
 
-        lax.fori_loop(0, (last - first) // 4, group, (here, flux))
+        lax.fori_loop(0, (last - first) // size, group, (here, flux))
 
     def deliveries(slot):
         result = []
@@ -399,7 +429,9 @@
             src_ref=into, dst_ref=into, send_sem=fin_send_sem.at[0],
             recv_sem=fin_recv_sem.at[source_tile], device_id=sibling, device_id_type=mesh_type)
         pl.when(tile != source_tile)(arrived.wait_recv)
-    out_ref[0] = finals[...]
+    matrix = one_hot(True)
+    for layer in range(4):
+        out_ref[0, layer] = moved(finals[layer], matrix)
 
 
 def window_body(initial, mobility):
@@ -420,6 +452,7 @@
             field, field,
             pltpu.VMEM((2, 8, 8, width), f32),
             pltpu.VMEM(initial.shape, f32),
+            pltpu.VMEM((2,) + initial.shape, f32),
             pltpu.SemaphoreType.DMA((4,)),
             pltpu.SemaphoreType.DMA((4,)),
             pltpu.SemaphoreType.DMA((4,)),

time: 49.4 us -> 33.6 us (0.68)
  Pallas kernels: 46.6 us -> 30.8 us
    pallas_call x1, Pallas kernels: 46.6 us -> 30.8 us  [window_body(): pl.pallas_call(functools.partial(window_kernel, weights), out_shape=jax.S...]
where the time goes in v2:
time: 33.6 us; the launch traced here: 33.4 us
  Pallas kernels  30.8 us (92%)
  local copies, waits for them, and re-layouts  2.6 us (8%)
    pallas_call x1, Pallas kernels, window_body(): pl.pallas_call(functools.partial(window_kernel, weights), out_shape=jax.S...  30.8 us
    unnamed x5, local copies, waits for them, and re-layouts  2.6 us

profile of v2, /device:TPU:1, one launch (start us, length us, event | category | flops | bytes accessed | tf_op | source)
XLA Modules:
  0.0 33.4 jit_solution(8401705194608654826)
XLA Ops:
  0.0 0.0 copy-start
  0.0 0.9 %copy-done = f32[4,32,512]{2,1,0:T(8,128)S(1)} copy-done((f32[4,32,512]{2,1,0:T(8,128)S(1)}, f32[4,32,512]{2,1,0:T(8,128)}, u32[]{:S(2)}) %copy-start) | copy-done | bytes 262168
  1.0 0.0 copy-start.1
  1.0 0.9 %copy-done.1 = f32[4,32,512]{2,1,0:T(8,128)S(1)} copy-done((f32[4,32,512]{2,1,0:T(8,128)S(1)}, f32[4,32,512]{2,1,0:T(8,128)}, u32[]{:S(2)}) %copy-start.1) | copy-done | bytes 262168
  1.9 30.8 %shard_map.28 = f32[1,4,32,512]{3,2,1,0:T(8,128)S(1)} custom-call(f32[4,32,512]{2,1,0:T(8,128)S(1)} %copy-done, f32[4,32,512]{2,1,0:T(8,128)S(1)} %copy-done.1), custom_call_target="tpu_custom_call" | custom-call | tf_op jit(solution)/shard_map/pallas_call | solution.py:442
  32.7 0.7 %copy.4 = f32[1,4,32,512]{3,2,1,0:T(8,128)} copy(f32[1,4,32,512]{3,2,1,0:T(8,128)S(1)} %shard_map.28) | data formatting | bytes 524288
Async XLA Ops:
  0.0 0.9 %copy-start = (f32[4,32,512]{2,1,0:T(8,128)S(1)}, f32[4,32,512]{2,1,0:T(8,128)}, u32[]{:S(2)}) copy-start(f32[4,32,512]{2,1,0:T(8,128)} %c_ref.1) | copy-start | bytes 786436
  1.0 0.9 %copy-start.1 = (f32[4,32,512]{2,1,0:T(8,128)S(1)}, f32[4,32,512]{2,1,0:T(8,128)}, u32[]{:S(2)}) copy-start(f32[4,32,512]{2,1,0:T(8,128)} %m_ref.1) | copy-start | bytes 786436

commit v3 on v2

--- a/solution.py
+++ b/solution.py
@@ -179,7 +179,9 @@
         partner = (level, 1 - gx, gy)
         row_to = 8 * jnp.maximum(2 - partner_tile, 0)
         return [
-            (None, copy(piece(8 * low, 24), region(array, gx, row_to, 24), 0, 0, partner)),
+            (None, copy(piece(8 * low, 8), region(array, gx, row_to, 8), 0, 0, partner)),
+            (None, copy(piece(8 * low + 8, 8), region(array, gx, row_to + 8, 8), 4, 4, partner)),
+            (None, copy(piece(8 * low + 16, 8), region(array, gx, row_to + 16, 8), 5, 5, partner)),
             (x == gx, copy(piece(24, 8), region(array, gx, jnp.where(x == gx, 8 * (5 - partner_tile), 0), 8), 1, 1, partner)),
             (x == 0, copy(piece(16, 16), region(array, gx, 0, 16), 2, 2 + gx, to_above)),
             (x == 1, copy(piece(24, 8), region(array, gx, 0, 8), 2, 2 + gx, to_above)),
@@ -208,7 +210,9 @@
 
         same = x == gx
         entries = [
-            (None, copy(1 - gx, 8 * jnp.maximum(2 - tile, 0), 24, 0)),
+            (None, copy(1 - gx, 8 * jnp.maximum(2 - tile, 0), 8, 0)),
+            (None, copy(1 - gx, 8 * jnp.maximum(2 - tile, 0) + 8, 8, 4)),
+            (None, copy(1 - gx, 8 * jnp.maximum(2 - tile, 0) + 16, 8, 5)),
             (jnp.logical_not(same), copy(1 - gx, jnp.where(same, 0, 8 * (5 - tile)), 8, 1)),
         ]
         for half, kind in ((gx, 2), (1 - gx, 3)):
@@ -295,26 +299,24 @@
             pieces = [pltpu.roll(pieces[-1], 1, 1)] + pieces[:-1]
         return jnp.concatenate(pieces, axis=1)
 
-    def turn(block, carry):
-        row = pl.multiple_of(8 * block, 8)
+    for row in range(0, 40, 8):
         for array, target in ((0, c0), (1, sol_a)):
             for lane in range(0, width, 128):
-                cells = raw[array, :, pl.ds(row, 8), lane:lane + 128]
-                target[pl.ds(row, 8), :, lane:lane + 128] = jnp.swapaxes(cells, 0, 1)
+                cells = raw[array, :, row:row + 8, lane:lane + 128]
+                target[row:row + 8, :, lane:lane + 128] = jnp.swapaxes(cells, 0, 1)
+
+    half_step = 0.5 * time_step
+
+    def faces(group, carry):
+        for offset in range(19):
+            row = 1 + 19 * group + offset
+            here = sol_a[row]
+            mx[row] = half_step * (here + roll_x(here, -1))
+            mz[row] = half_step * (here + roll_z(here, -1))
+            my[row] = half_step * (here + sol_a[row + 1])
         return carry
 
-    lax.fori_loop(0, 5, turn, 0)
-
-    half_step = 0.5 * time_step
-
-    def faces(row, carry):
-        here = sol_a[row]
-        mx[row] = half_step * (here + roll_x(here, -1))
-        mz[row] = half_step * (here + roll_z(here, -1))
-        my[row] = half_step * (here + sol_a[row + 1])
-        return carry
-
-    lax.fori_loop(1, 39, faces, 0)
+    lax.fori_loop(0, 2, faces, 0)
 
     def potential(state, row):
         centre = state[row]
@@ -453,10 +455,10 @@
             pltpu.VMEM((2, 8, 8, width), f32),
             pltpu.VMEM(initial.shape, f32),
             pltpu.VMEM((2,) + initial.shape, f32),
-            pltpu.SemaphoreType.DMA((4,)),
-            pltpu.SemaphoreType.DMA((4,)),
-            pltpu.SemaphoreType.DMA((4,)),
-            pltpu.SemaphoreType.DMA((4,)),
+            pltpu.SemaphoreType.DMA((6,)),
+            pltpu.SemaphoreType.DMA((6,)),
+            pltpu.SemaphoreType.DMA((6,)),
+            pltpu.SemaphoreType.DMA((6,)),
             pltpu.SemaphoreType.DMA((2, 2)),
             pltpu.SemaphoreType.DMA((4,)),
             pltpu.SemaphoreType.DMA((4,)),

time: 33.6 us -> 31 us (0.923)
  Pallas kernels: 30.8 us -> 28.2 us
    pallas_call x1, Pallas kernels: 30.8 us -> 28.2 us  [window_body(): pl.pallas_call(functools.partial(window_kernel, weights), out_shape=jax.S...]
where the time goes in v3:
time: 31 us; the launch traced here: 30.8 us
  Pallas kernels  28.2 us (91%)
  local copies, waits for them, and re-layouts  2.6 us (8%)
    pallas_call x1, Pallas kernels, window_body(): pl.pallas_call(functools.partial(window_kernel, weights), out_shape=jax.S...  28.2 us
    unnamed x5, local copies, waits for them, and re-layouts  2.6 us

profile of v3, /device:TPU:1, one launch (start us, length us, event | category | flops | bytes accessed | tf_op | source)
XLA Modules:
  0.0 30.8 jit_solution(5853539311664382966)
XLA Ops:
  0.0 0.0 copy-start
  0.0 0.9 %copy-done = f32[4,32,512]{2,1,0:T(8,128)S(1)} copy-done((f32[4,32,512]{2,1,0:T(8,128)S(1)}, f32[4,32,512]{2,1,0:T(8,128)}, u32[]{:S(2)}) %copy-start) | copy-done | bytes 262168
  1.0 0.0 copy-start.1
  1.0 0.9 %copy-done.1 = f32[4,32,512]{2,1,0:T(8,128)S(1)} copy-done((f32[4,32,512]{2,1,0:T(8,128)S(1)}, f32[4,32,512]{2,1,0:T(8,128)}, u32[]{:S(2)}) %copy-start.1) | copy-done | bytes 262168
  1.9 28.2 %shard_map.28 = f32[1,4,32,512]{3,2,1,0:T(8,128)S(1)} custom-call(f32[4,32,512]{2,1,0:T(8,128)S(1)} %copy-done, f32[4,32,512]{2,1,0:T(8,128)S(1)} %copy-done.1), custom_call_target="tpu_custom_call" | custom-call | tf_op jit(solution)/shard_map/pallas_call | solution.py:444
  30.1 0.7 %copy.4 = f32[1,4,32,512]{3,2,1,0:T(8,128)} copy(f32[1,4,32,512]{3,2,1,0:T(8,128)S(1)} %shard_map.28) | data formatting | bytes 524288
Async XLA Ops:
  0.0 0.9 %copy-start = (f32[4,32,512]{2,1,0:T(8,128)S(1)}, f32[4,32,512]{2,1,0:T(8,128)}, u32[]{:S(2)}) copy-start(f32[4,32,512]{2,1,0:T(8,128)} %c_ref.1) | copy-start | bytes 786436
  1.0 0.9 %copy-start.1 = (f32[4,32,512]{2,1,0:T(8,128)S(1)}, f32[4,32,512]{2,1,0:T(8,128)}, u32[]{:S(2)}) copy-start(f32[4,32,512]{2,1,0:T(8,128)} %m_ref.1) | copy-start | bytes 786436

commit v4 on v3

--- a/solution.py
+++ b/solution.py
@@ -135,10 +135,16 @@
     return solution[None]
 
 
-def window_kernel(weights, c_ref, m_ref, out_ref, raw, c0, mx, my, mz, rates_a, rates_b, sol_a, sol_b,
+def window_kernel(weights, c_hbm, m_hbm, out_ref, fields, in_sem, raw, c0, mx, my, mz, rates_a, rates_b, sol_a, sol_b,
                   ready, finals, stage, send_sem, recv_sem, fwd_send_sem, fwd_recv_sem, own_sem,
                   fin_send_sem, fin_recv_sem, fin_own_sem):
     steps = len(weights)
+    fetched = [
+        pltpu.make_async_copy(source, fields.at[array], in_sem.at[array])
+        for array, source in enumerate((c_hbm, m_hbm))
+    ]
+    for copy in fetched:
+        copy.start()
     level = lax.axis_index("level")
     gx = lax.axis_index("gx")
     gy = lax.axis_index("gy")
@@ -231,7 +237,7 @@
                 own_sem.at[array, 1])),
         ]
 
-    width = c_ref.shape[2]
+    width = c_hbm.shape[2]
     parts = width // 128
 
     def one_hot(inverse):
@@ -248,21 +254,23 @@
         taken = [jnp.dot(part, matrix, preferred_element_type=jnp.float32) for part in (high, middle, low)]
         return (taken[0] + taken[1]) + taken[2]
 
-    def interleave(array, source):
-        matrix = one_hot(False)
+    matrix_in = one_hot(False)
+
+    def interleave(array):
+        fetched[array].wait()
         for layer in range(4):
-            stage[array, layer] = moved(source[layer], matrix)
-
-    for array, source in enumerate((c_ref, m_ref)):
-        pl.when(core == array)(functools.partial(interleave, array, source))
+            stage[array, layer] = moved(fields[array, layer], matrix_in)
+
+    for array in range(2):
+        pl.when(core == array)(functools.partial(interleave, array))
     pl.semaphore_wait(barrier, len(greeted))
     for array in range(2):
         @pl.when(core == array)
         def _(array=array):
             for condition, copy in outgoing(array, stage.at[array]):
                 when(condition, copy.start)
-    for array, source in enumerate((c_ref, m_ref)):
-        pl.when(core != array)(functools.partial(interleave, array, source))
+    for array in range(2):
+        pl.when(core != array)(functools.partial(interleave, array))
     staged = (stage.at[0], stage.at[1])
     for array, source in enumerate(staged):
         for condition, copy in own(array, source):
@@ -444,9 +452,11 @@
     return pl.pallas_call(
         functools.partial(window_kernel, weights),
         out_shape=jax.ShapeDtypeStruct((1,) + initial.shape, f32),
-        in_specs=[pl.BlockSpec(memory_space=pltpu.VMEM)] * 2,
+        in_specs=[pl.BlockSpec(memory_space=pltpu.HBM)] * 2,
         out_specs=pl.BlockSpec(memory_space=pltpu.VMEM),
         scratch_shapes=[
+            pltpu.VMEM((2,) + initial.shape, f32),
+            pltpu.SemaphoreType.DMA((2,)),
             pltpu.VMEM((2, 8, 40, width), f32),
             field, field, field, field,
             pltpu.VMEM((STEPS + 1, 40, 8, width), f32),
@@ -465,7 +475,7 @@
             pltpu.SemaphoreType.DMA,
         ],
         compiler_params=pltpu.CompilerParams(
-            collective_id=0, has_side_effects=True, vmem_limit_bytes=40 * 1024 * 1024
+            collective_id=0, has_side_effects=True, vmem_limit_bytes=66322432
         ),
     )(initial, mobility)
 

time: 31 us -> 30.8 us (level)
  local copies, waits for them, and re-layouts: 2.6 us -> 1.67 us
  Pallas kernels: 28.2 us -> 29 us
    unnamed x5 -> x1, local copies, waits for them, and re-layouts: 2.6 us -> 1.67 us
    pallas_call x1, Pallas kernels: 28.2 us -> 29 us  [window_body(): pl.pallas_call(functools.partial(window_kernel, weights), out_shape=jax.S...]
where the time goes in v4:
time: 30.8 us; the launch traced here: 30.6 us
  Pallas kernels  29 us (94%)
  local copies, waits for them, and re-layouts  1.67 us (5%)
    pallas_call x1, Pallas kernels, window_body(): pl.pallas_call(functools.partial(window_kernel, weights), out_shape=jax.S...  29 us
    unnamed x1, local copies, waits for them, and re-layouts  1.67 us

profile of v4, /device:TPU:1, one launch (start us, length us, event | category | flops | bytes accessed | tf_op | source)
XLA Modules:
  0.0 30.6 jit_solution(3508494830897996830)
XLA Ops:
  0.0 29.0 %shard_map.28 = f32[1,4,32,512]{3,2,1,0:T(8,128)} custom-call(f32[4,32,512]{2,1,0:T(8,128)} %c_hbm.1, f32[4,32,512]{2,1,0:T(8,128)} %m_hbm.1), custom_call_target="tpu_custom_call" | custom-call | tf_op jit(solution)/shard_map/pallas_call | solution.py:452
  29.0 1.7 %copy.4 = f32[1,4,32,512]{3,2,1,0:T(8,128)} copy(f32[1,4,32,512]{3,2,1,0:T(8,128)} %shard_map.28) | data formatting | bytes 524288
